TPU v7x, 512 devices: a whole 4x4x16 slice. The times are simulated.
512 devices in a mesh: row: 8 (over z_lo), col: 16 (over x, y), layer: 4 (over z_hi, core).
Axes of the slice: x: 4, y: 4, z: 16 (z_hi: 2, z_lo: 8; z = z_hi * 8 + z_lo), core: 2. Of those that a mesh axis runs over, the one named last changes fastest.
Arguments:
- doubles_amplitude_tensor: float32 [2304, 2048], P('col', 'layer'), may hold values from -6 to 6
- integrals: float32 [8, 16, 4, 96, 2048], P('row', 'col', 'layer'), may hold values from -0.125 to 0.125
- incoming_residual: float32 [2304, 49152], P('col', ('row', 'layer')), may hold values from -6 to 6
Outputs:
- updated_residual: float32 [2304, 49152], P('col', ('row', 'layer'))
All inputs are finite; a program needn't handle non-finite values.
Results may differ from a plain program's by a relative error of at most 0.00005.
Values sent between devices are 32-bit elements; how exact they have to be, the bound alone decides.
No kernel may reach another device: no remote copies, remote signals or barrier semaphores. Data moves between devices by JAX's collectives and lax.ppermute only.
A program may use at most 64 MiB of HBM per device.

v0:
```python
import jax
import jax.numpy as jnp
from jax import lax
from jax.sharding import PartitionSpec as P


def regroup(integrals):
    local = integrals.reshape(1, integrals.shape[3], integrals.shape[4])
    return lax.all_to_all(local, "layer", split_axis=2, concat_axis=0, tiled=True)


def on_device(doubles_amplitude_tensor, integrals, incoming_residual):
    ij_rows = doubles_amplitude_tensor.shape[0]
    regrouped = regroup(integrals)[None]
    partial_ladder_value = jnp.einsum(
        "ic,nlkc->inlk",
        doubles_amplitude_tensor,
        lax.all_gather(regrouped, "col", axis=0, tiled=True),
        precision=lax.Precision.HIGHEST,
        preferred_element_type=jnp.float32,
    )
    summed = lax.psum_scatter(partial_ladder_value, "layer", scatter_dimension=2, tiled=True)
    return incoming_residual + summed.reshape(ij_rows, -1)


def solution(mesh):
    return jax.shard_map(
        on_device,
        mesh=mesh,
        in_specs=(
            P("col", "layer"),
            P("row", "col", "layer", None, None),
            P("col", ("row", "layer")),
        ),
        out_specs=P("col", ("row", "layer")),
        check_vma=False,
    )
```

profile of v0, /device:TPU:1, one launch (start us, length us, event | category | flops | bytes accessed | tf_op | source)
XLA Modules:
  0.0 565.8 jit_solution(12398285052435293716)
XLA Ops:
  6.5 0.0 copy-start
  6.5 0.0 all-gather.3.cloned.1.call-start
  6.5 1.5 copy.7
  8.1 43.3 %all_to_all.15 = f32[1,96,2048]{1,0,2:T(1,128)S(1)} all-to-all(f32[1,96,2048]{1,0,2:T(1,128)S(1)} %bitcast.24), channel_id=1, replica_groups=mesh['row'=8,'col'=16,'layer'=4] {'layer'}, dimensions={2} | all-to-all | bytes 1572864 | tf_op jit(solution)/shard_map/all_to_all | solution.py:9
  51.4 1.2 copy.8
  52.6 0.0 all-gather.3.cloned.1.call-update
  52.6 0.0 all-reduce.3.cloned.1.call-start
  52.6 128.7 %all-gather.3.cloned.1.call-done = f32[64,1,96,512]{3,2,1,0:T(8,128)} async-done(((f32[4,1,96,512]{3,2,1,0:T(8,128)}), f32[64,1,96,512]{3,2,1,0:T(8,128)}) %all-gather.3.cloned.1.call-update) | async-done | bytes 12582928 | tf_op jit(solution)/shard_map/all_gather | solution.py:18
  181.3 0.0 copy-done
  181.4 18.7 %fusion = f32[144,16,4,96]{3,0,2,1:T(8,128)} fusion(f32[144,512]{1,0:T(8,128)S(1)} %copy-done, f32[16,4,96,512]{3,2,1,0:T(8,128)} %bitcast.22), kind=kOutput, calls=%fused_computation | convolution fusion | flops 5435817984 | bytes 16416768 | tf_op jit(solution)/shard_map/ic,nlkc->inlk/dot_general | solution.py:15
  200.1 0.0 copy-start.1
  200.1 0.0 all-reduce.3.cloned.1.call-update
  200.1 1.3 dynamic-slice
  201.5 353.6 %all-reduce.3.cloned.1.call-done = f32[144,16,4,96]{3,0,2,1:T(8,128)} async-done(((f32[144,16,4,96]{3,0,2,1:T(8,128)}), f32[144,16,4,96]{3,0,2,1:T(8,128)}) %all-reduce.3.cloned.1.call-update) | async-done | bytes 3538960
  555.1 2.0 constant_dynamic-slice_fusion
  557.1 0.4 copy.9
  557.5 0.5 reshape.8
  558.0 0.0 copy-done.1
  558.0 1.0 add.5
Async XLA Ops:
  6.5 174.8 %copy-start = (f32[144,512]{1,0:T(8,128)S(1)}, f32[144,512]{1,0:T(8,128)}, u32[]{:S(2)}) copy-start(f32[144,512]{1,0:T(8,128)} %param.3) | copy-start | bytes 884740
  6.5 174.8 %all-gather.3.cloned.1.call-start = ((), (), s32[]{:S(2)}) async-start(), calls=%async_computation.1 | async-start | bytes 13369344 | tf_op jit(solution)/shard_map/all_gather | solution.py:18
  52.6 502.5 %all-reduce.3.cloned.1.call-start = ((), (), s32[]{:S(2)}) async-start(), calls=%async_computation.2 | async-start | bytes 9437184
  200.1 357.9 %copy-start.1 = (f32[144,1536]{1,0:T(8,128)S(1)}, f32[144,1536]{1,0:T(8,128)}, u32[]{:S(2)}) copy-start(f32[144,1536]{1,0:T(8,128)} %param.5) | copy-start | bytes 2654212
Sparse Core Ops, SparseCore 0:
  52.7 128.5 all-gather.2
  200.2 354.7 all-reduce.2
where the time goes:
time: 566 us
  waiting for transfers between devices  482 us (85%)
  blocking collectives  43.3 us (8%)
  matrix products  18.7 us (3%)
  between operations  13.4 us (2%)
  local copies, waits for them, and re-layouts  6.95 us (1%)
    unnamed x3, waiting for transfers between devices  354 us
    all_gather x1, waiting for transfers between devices, on_device(): lax.all_gather(regrouped, 'col', axis=0, tiled=True)  129 us
    all_to_all x1, blocking collectives, regroup(): lax.all_to_all(local, 'layer', split_axis=2, concat_axis=0, tiled=True)  43.3 us
    dot_general x1, matrix products, on_device(): jnp.einsum('ic,nlkc->inlk', doubles_amplitude_tensor, lax.all_gather(regr...  18.7 us
  transfers between devices with their start and end apart: 2, of which 2 were waited for; matrix products, arithmetic and copies ran while one was open for 0% of the time, Pallas kernels for 0%

commit v1 on v0

--- a/solution.py
+++ b/solution.py
@@ -2,6 +2,34 @@
 import jax.numpy as jnp
 from jax import lax
 from jax.sharding import PartitionSpec as P
+
+
+def view_blocks_on(mine, dim_at):
+    mine = jnp.moveaxis(mine, 0, dim_at)
+    lower = mine.shape
+    local_next = mine.reshape(
+        *lower[:dim_at], lower[dim_at] * lower[dim_at + 1], *lower[dim_at + 2 :]
+    )
+    return local_next
+
+
+def divide_the_islands(panel, which_axis, axis_k):
+    devs = lax.axis_size(which_axis)
+    log = [(kk, (kk + 1) % devs) for kk in range(devs)]
+    piece_out, response = ([], [])
+    dev_i = 0
+    frames = [(s, ii) for ii, s in log]
+    while dev_i < devs - 1:
+        if dev_i % 2 == 0:
+            piece_out.append(lax.ppermute(piece_out[-1] if piece_out else panel, which_axis, log))
+        else:
+            response.append(lax.ppermute(response[-1] if response else panel, which_axis, frames))
+        dev_i = dev_i + 1
+    formed = jnp.stack([*piece_out[::-1], panel, *response])
+    current_arr = lax.axis_index(which_axis) - len(piece_out)
+    formed = formed[(jnp.arange(devs) - current_arr) % devs]
+    prior = view_blocks_on(formed, axis_k)
+    return prior
 
 
 def regroup(integrals):
@@ -15,7 +43,7 @@
     partial_ladder_value = jnp.einsum(
         "ic,nlkc->inlk",
         doubles_amplitude_tensor,
-        lax.all_gather(regrouped, "col", axis=0, tiled=True),
+        divide_the_islands(regrouped, "col", 0),
         precision=lax.Precision.HIGHEST,
         preferred_element_type=jnp.float32,
     )

time: 566 us -> 662 us (1.17)
  starting transfers between devices: 0.04 us -> 65.9 us
  local copies, waits for them, and re-layouts: 6.95 us -> 44.5 us
  waiting for transfers between devices: 482 us -> 473 us
    all_gather x1 -> x0, waiting for transfers between devices: 129 us -> none  [on_device(): lax.all_gather(regrouped, 'col', axis=0, tiled=True)]
    ppermute x0 -> x15, waiting for transfers between devices: none -> 93.3 us  [the longest x8 92.1 us: divide_the_islands(): lax.ppermute(piece_out[-1] if piece_out else panel, which_axis, log)]
    ppermute x0 -> x15, starting transfers between devices: none -> 65.9 us  [the longest x7 49.3 us: divide_the_islands(): lax.ppermute(response[-1] if response else panel, which_axis, frames)]
    unnamed x7 -> x38, local copies, waits for them, and re-layouts: 4.85 us -> 31.9 us
    unnamed x3 -> x2, waiting for transfers between devices: 354 us -> 380 us
    gather x0 -> x1, local copies, waits for them, and re-layouts: none -> 10.4 us  [divide_the_islands(): formed = formed[(jnp.arange(devs) - current_arr) % devs]]
  transfers between devices with their start and end apart: 2 -> 16, of which waited for: 2 -> 11; matrix products, arithmetic and copies ran while one was open for 0% -> 4% of each run, Pallas kernels for 0% -> 0%
where the time goes in v1:
time: 662 us; the launch traced here: 661 us
  waiting for transfers between devices  473 us (71%)
  starting transfers between devices  65.9 us (10%)
  local copies, waits for them, and re-layouts  44.5 us (7%)
  blocking collectives  43.3 us (7%)
  matrix products  19.3 us (3%)
  between operations  13.7 us (2%)
    unnamed x2, waiting for transfers between devices  380 us
    ppermute x8, waiting for transfers between devices, divide_the_islands(): lax.ppermute(piece_out[-1] if piece_out else panel, which_axis, log)  92.1 us
    ppermute x7, starting transfers between devices, divide_the_islands(): lax.ppermute(response[-1] if response else panel, which_axis, frames)  49.3 us
    all_to_all x1, blocking collectives, regroup(): lax.all_to_all(local, 'layer', split_axis=2, concat_axis=0, tiled=True)  43.3 us
    unnamed x38, local copies, waits for them, and re-layouts  31.9 us
    dot_general x1, matrix products, on_device(): jnp.einsum('ic,nlkc->inlk', doubles_amplitude_tensor, divide_the_islands(...  19.3 us
    ppermute x8, starting transfers between devices, divide_the_islands(): lax.ppermute(piece_out[-1] if piece_out else panel, which_axis, log)  16.6 us
  transfers between devices with their start and end apart: 16, of which 11 were waited for; matrix products, arithmetic and copies ran while one was open for 4% of the time, Pallas kernels for 0%

profile of v1, /device:TPU:1, one launch (start us, length us, event | category | flops | bytes accessed | tf_op | source)
XLA Modules:
  0.0 661.2 jit_solution(11391801111458867324)
XLA Ops:
  8.1 43.3 %all_to_all.15 = f32[1,96,2048]{1,0,2:T(1,128)S(1)} all-to-all(f32[1,96,2048]{1,0,2:T(1,128)S(1)} %bitcast.89), channel_id=1, replica_groups=mesh['row'=8,'col'=16,'layer'=4] {'layer'}, dimensions={2} | all-to-all | bytes 1572864 | tf_op jit(solution)/shard_map/all_to_all | solution.py:37
  51.7 3.2 collective-permute-start
  54.9 20.3 %collective-permute-done = f32[1,4,96,512]{3,2,1,0:T(8,128)S(1)} collective-permute-done((f32[1,4,96,512]{3,2,1,0:T(8,128)S(1)}, f32[1,4,96,512]{3,2,1,0:T(8,128)S(1)}, u32[]{:S(2)}, u32[]{:S(2)}) %collective-permute-start) | collective-permute-done | bytes 786464 | tf_op jit(solution)/shard_map/ppermute | solution.py:24
  77.1 6.7 %collective-permute-start.8 = (f32[1,4,96,512]{3,2,1,0:T(8,128)S(1)}, f32[1,4,96,512]{3,2,1,0:T(8,128)S(1)}, u32[]{:S(2)}, u32[]{:S(2)}) collective-permute-start(f32[1,4,96,512]{3,2,1,0:T(8,128)S(1)} %bitcast.91), channel_id=1, source_target_pairs={{4,0},{8,4},{12,8},{16,12},{20,16},{24,20},{28,24},{32,28},{36,32}... | collective-permute-start | bytes 2359304 | tf_op jit(solution)/shard_map/ppermute | solution.py:26
  83.8 13.9 %collective-permute-done.1 = f32[1,4,96,512]{3,2,1,0:T(8,128)} collective-permute-done((f32[1,4,96,512]{3,2,1,0:T(8,128)S(1)}, f32[1,4,96,512]{3,2,1,0:T(8,128)}, u32[]{:S(2)}, u32[]{:S(2)}) %collective-permute-start.1) | collective-permute-done | bytes 786464 | tf_op jit(solution)/shard_map/ppermute | solution.py:24
  99.6 6.7 %collective-permute-start.9 = (f32[1,4,96,512]{3,2,1,0:T(8,128)S(1)}, f32[1,4,96,512]{3,2,1,0:T(8,128)S(1)}, u32[]{:S(2)}, u32[]{:S(2)}) collective-permute-start(f32[1,4,96,512]{3,2,1,0:T(8,128)S(1)} %collective-permute-done.8), channel_id=1, source_target_pairs={{4,0},{8,4},{12,8},{16,12},{20,16},{24,20},{28,24},{32,28},{36,32}... | collective-permute-start | bytes 2359304 | tf_op jit(solution)/shard_map/ppermute | solution.py:26
  106.3 13.2 %collective-permute-done.2 = f32[1,4,96,512]{3,2,1,0:T(8,128)} collective-permute-done((f32[1,4,96,512]{3,2,1,0:T(8,128)}, f32[1,4,96,512]{3,2,1,0:T(8,128)}, u32[]{:S(2)}, u32[]{:S(2)}) %collective-permute-start.2) | collective-permute-done | bytes 786464 | tf_op jit(solution)/shard_map/ppermute | solution.py:24
  122.2 6.7 %collective-permute-start.10 = (f32[1,4,96,512]{3,2,1,0:T(8,128)S(1)}, f32[1,4,96,512]{3,2,1,0:T(8,128)S(1)}, u32[]{:S(2)}, u32[]{:S(2)}) collective-permute-start(f32[1,4,96,512]{3,2,1,0:T(8,128)S(1)} %collective-permute-done.9), channel_id=1, source_target_pairs={{4,0},{8,4},{12,8},{16,12},{20,16},{24,20},{28,24},{32,28},{36,32}... | collective-permute-start | bytes 2359304 | tf_op jit(solution)/shard_map/ppermute | solution.py:26
  128.9 11.3 %collective-permute-done.3 = f32[1,4,96,512]{3,2,1,0:T(8,128)} collective-permute-done((f32[1,4,96,512]{3,2,1,0:T(8,128)}, f32[1,4,96,512]{3,2,1,0:T(8,128)}, u32[]{:S(2)}, u32[]{:S(2)}) %collective-permute-start.3) | collective-permute-done | bytes 786464 | tf_op jit(solution)/shard_map/ppermute | solution.py:24
  143.1 7.0 %collective-permute-start.11 = (f32[1,4,96,512]{3,2,1,0:T(8,128)S(1)}, f32[1,4,96,512]{3,2,1,0:T(8,128)S(1)}, u32[]{:S(2)}, u32[]{:S(2)}) collective-permute-start(f32[1,4,96,512]{3,2,1,0:T(8,128)S(1)} %collective-permute-done.10), channel_id=1, source_target_pairs={{4,0},{8,4},{12,8},{16,12},{20,16},{24,20},{28,24},{32,28},{36,32}... | collective-permute-start | bytes 2359304 | tf_op jit(solution)/shard_map/ppermute | solution.py:26
  150.1 10.0 %collective-permute-done.4 = f32[1,4,96,512]{3,2,1,0:T(8,128)S(1)} collective-permute-done((f32[1,4,96,512]{3,2,1,0:T(8,128)}, f32[1,4,96,512]{3,2,1,0:T(8,128)S(1)}, u32[]{:S(2)}, u32[]{:S(2)}) %collective-permute-start.4) | collective-permute-done | bytes 786464 | tf_op jit(solution)/shard_map/ppermute | solution.py:24
  162.9 7.4 %collective-permute-start.12 = (f32[1,4,96,512]{3,2,1,0:T(8,128)S(1)}, f32[1,4,96,512]{3,2,1,0:T(8,128)}, u32[]{:S(2)}, u32[]{:S(2)}) collective-permute-start(f32[1,4,96,512]{3,2,1,0:T(8,128)S(1)} %collective-permute-done.11), channel_id=1, source_target_pairs={{4,0},{8,4},{12,8},{16,12},{20,16},{24,20},{28,24},{32,28},{36,32}... | collective-permute-start | bytes 2359304 | tf_op jit(solution)/shard_map/ppermute | solution.py:26
  170.3 8.5 %collective-permute-done.5 = f32[1,4,96,512]{3,2,1,0:T(8,128)S(1)} collective-permute-done((f32[1,4,96,512]{3,2,1,0:T(8,128)S(1)}, f32[1,4,96,512]{3,2,1,0:T(8,128)S(1)}, u32[]{:S(2)}, u32[]{:S(2)}) %collective-permute-start.5) | collective-permute-done | bytes 786464 | tf_op jit(solution)/shard_map/ppermute | solution.py:24
  181.3 7.5 %collective-permute-start.13 = (f32[1,4,96,512]{3,2,1,0:T(8,128)}, f32[1,4,96,512]{3,2,1,0:T(8,128)}, u32[]{:S(2)}, u32[]{:S(2)}) collective-permute-start(f32[1,4,96,512]{3,2,1,0:T(8,128)} %collective-permute-done.12), channel_id=1, source_target_pairs={{4,0},{8,4},{12,8},{16,12},{20,16},{24,20},{28,24},{32,28},{36,32}... | collective-permute-start | bytes 2359304 | tf_op jit(solution)/shard_map/ppermute | solution.py:26
  188.8 7.8 %collective-permute-done.6 = f32[1,4,96,512]{3,2,1,0:T(8,128)} collective-permute-done((f32[1,4,96,512]{3,2,1,0:T(8,128)S(1)}, f32[1,4,96,512]{3,2,1,0:T(8,128)}, u32[]{:S(2)}, u32[]{:S(2)}) %collective-permute-start.6) | collective-permute-done | bytes 786464 | tf_op jit(solution)/shard_map/ppermute | solution.py:24
  199.2 7.4 %collective-permute-start.14 = (f32[1,4,96,512]{3,2,1,0:T(8,128)}, f32[1,4,96,512]{3,2,1,0:T(8,128)S(1)}, u32[]{:S(2)}, u32[]{:S(2)}) collective-permute-start(f32[1,4,96,512]{3,2,1,0:T(8,128)} %collective-permute-done.13), channel_id=1, source_target_pairs={{4,0},{8,4},{12,8},{16,12},{20,16},{24,20},{28,24},{32,28},{36,32}... | collective-permute-start | bytes 2359304 | tf_op jit(solution)/shard_map/ppermute | solution.py:26
  206.6 7.2 %collective-permute-done.7 = f32[1,4,96,512]{3,2,1,0:T(8,128)} collective-permute-done((f32[1,4,96,512]{3,2,1,0:T(8,128)}, f32[1,4,96,512]{3,2,1,0:T(8,128)}, u32[]{:S(2)}, u32[]{:S(2)}) %collective-permute-start.7) | collective-permute-done | bytes 786464 | tf_op jit(solution)/shard_map/ppermute | solution.py:24
  215.9 2.1 bitcast_dynamic-update-slice_fusion.13
  220.1 2.1 bitcast_dynamic-update-slice_fusion.11
  222.1 2.1 bitcast_dynamic-update-slice_fusion.10
  226.3 2.1 bitcast_dynamic-update-slice_fusion.8
  239.2 10.4 %gather_fusion = f32[16,4,96,512]{3,2,1,0:T(8,128)} fusion(f32[16,4,96,512]{3,2,1,0:T(8,128)} %bitcast.36, s32[1024]{0:T(1024)S(1)} %pad_clamp_fusion), kind=kCustom, calls=%fused_computation | custom fusion | bytes 25165888 | tf_op jit(solution)/shard_map/gather | solution.py:30
  249.6 19.3 %convolution_bitcast_fusion = f32[144,16,4,96]{3,0,2,1:T(8,128)} fusion(f32[16,4,96,512]{3,2,1,0:T(8,128)} %gather_fusion, f32[144,512]{1,0:T(8,128)S(1)} %copy-done), kind=kOutput, calls=%fused_computation.1 | convolution fusion | flops 5435817984 | bytes 16416768 | tf_op jit(solution)/shard_map/ic,nlkc->inlk/dot_general | solution.py:43
  270.3 380.2 %all-reduce.3.cloned.1.call-done = f32[144,16,4,96]{3,0,2,1:T(8,128)} async-done(((f32[144,16,4,96]{3,0,2,1:T(8,128)}), f32[144,16,4,96]{3,0,2,1:T(8,128)}) %all-reduce.3.cloned.1.call-update) | async-done | bytes 3538960
  (57 shorter events, 41.3 us)
Async XLA Ops:
  6.5 243.1 %copy-start = (f32[144,512]{1,0:T(8,128)S(1)}, f32[144,512]{1,0:T(8,128)}, u32[]{:S(2)}) copy-start(f32[144,512]{1,0:T(8,128)} %param.3) | copy-start | bytes 884740
  6.5 643.9 %all-reduce.3.cloned.1.call-start = ((), (), s32[]{:S(2)}) async-start(), calls=%async_computation.1 | async-start | bytes 9437184
  51.7 23.5 %collective-permute-start = (f32[1,4,96,512]{3,2,1,0:T(8,128)S(1)}, f32[1,4,96,512]{3,2,1,0:T(8,128)S(1)}, u32[]{:S(2)}, u32[]{:S(2)}) collective-permute-start(f32[1,4,96,512]{3,2,1,0:T(8,128)S(1)} %bitcast.90), channel_id=1, source_target_pairs={{0,4},{4,8},{8,12},{12,16},{16,20},{20,24},{24,28},{28,32},{32,36}... | collective-permute-start | bytes 2359304 | tf_op jit(solution)/shard_map/ppermute | solution.py:24
  75.2 22.5 %collective-permute-start.1 = (f32[1,4,96,512]{3,2,1,0:T(8,128)S(1)}, f32[1,4,96,512]{3,2,1,0:T(8,128)}, u32[]{:S(2)}, u32[]{:S(2)}) collective-permute-start(f32[1,4,96,512]{3,2,1,0:T(8,128)S(1)} %collective-permute-done), channel_id=1, source_target_pairs={{0,4},{4,8},{8,12},{12,16},{16,20},{20,24},{24,28},{28,32},{32,36}... | collective-permute-start | bytes 2359304 | tf_op jit(solution)/shard_map/ppermute | solution.py:24
  77.1 22.5 %collective-permute-start.8 = (f32[1,4,96,512]{3,2,1,0:T(8,128)S(1)}, f32[1,4,96,512]{3,2,1,0:T(8,128)S(1)}, u32[]{:S(2)}, u32[]{:S(2)}) collective-permute-start(f32[1,4,96,512]{3,2,1,0:T(8,128)S(1)} %bitcast.91), channel_id=1, source_target_pairs={{4,0},{8,4},{12,8},{16,12},{20,16},{24,20},{28,24},{32,28},{36,32}... | collective-permute-start | bytes 2359304 | tf_op jit(solution)/shard_map/ppermute | solution.py:26
  97.6 21.8 %collective-permute-start.2 = (f32[1,4,96,512]{3,2,1,0:T(8,128)}, f32[1,4,96,512]{3,2,1,0:T(8,128)}, u32[]{:S(2)}, u32[]{:S(2)}) collective-permute-start(f32[1,4,96,512]{3,2,1,0:T(8,128)} %collective-permute-done.1), channel_id=1, source_target_pairs={{0,4},{4,8},{8,12},{12,16},{16,20},{20,24},{24,28},{28,32},{32,36}... | collective-permute-start | bytes 2359304 | tf_op jit(solution)/shard_map/ppermute | solution.py:24
  99.6 21.8 %collective-permute-start.9 = (f32[1,4,96,512]{3,2,1,0:T(8,128)S(1)}, f32[1,4,96,512]{3,2,1,0:T(8,128)S(1)}, u32[]{:S(2)}, u32[]{:S(2)}) collective-permute-start(f32[1,4,96,512]{3,2,1,0:T(8,128)S(1)} %collective-permute-done.8), channel_id=1, source_target_pairs={{4,0},{8,4},{12,8},{16,12},{20,16},{24,20},{28,24},{32,28},{36,32}... | collective-permute-start | bytes 2359304 | tf_op jit(solution)/shard_map/ppermute | solution.py:26
  119.4 20.9 %collective-permute-start.3 = (f32[1,4,96,512]{3,2,1,0:T(8,128)}, f32[1,4,96,512]{3,2,1,0:T(8,128)}, u32[]{:S(2)}, u32[]{:S(2)}) collective-permute-start(f32[1,4,96,512]{3,2,1,0:T(8,128)} %collective-permute-done.2), channel_id=1, source_target_pairs={{0,4},{4,8},{8,12},{12,16},{16,20},{20,24},{24,28},{28,32},{32,36}... | collective-permute-start | bytes 2359304 | tf_op jit(solution)/shard_map/ppermute | solution.py:24
  122.2 19.9 %collective-permute-start.10 = (f32[1,4,96,512]{3,2,1,0:T(8,128)S(1)}, f32[1,4,96,512]{3,2,1,0:T(8,128)S(1)}, u32[]{:S(2)}, u32[]{:S(2)}) collective-permute-start(f32[1,4,96,512]{3,2,1,0:T(8,128)S(1)} %collective-permute-done.9), channel_id=1, source_target_pairs={{4,0},{8,4},{12,8},{16,12},{20,16},{24,20},{28,24},{32,28},{36,32}... | collective-permute-start | bytes 2359304 | tf_op jit(solution)/shard_map/ppermute | solution.py:26
  140.3 19.8 %collective-permute-start.4 = (f32[1,4,96,512]{3,2,1,0:T(8,128)}, f32[1,4,96,512]{3,2,1,0:T(8,128)S(1)}, u32[]{:S(2)}, u32[]{:S(2)}) collective-permute-start(f32[1,4,96,512]{3,2,1,0:T(8,128)} %collective-permute-done.3), channel_id=1, source_target_pairs={{0,4},{4,8},{8,12},{12,16},{16,20},{20,24},{24,28},{28,32},{32,36}... | collective-permute-start | bytes 2359304 | tf_op jit(solution)/shard_map/ppermute | solution.py:24
  142.2 0.9 copy-start.4
  143.1 18.9 %collective-permute-start.11 = (f32[1,4,96,512]{3,2,1,0:T(8,128)S(1)}, f32[1,4,96,512]{3,2,1,0:T(8,128)S(1)}, u32[]{:S(2)}, u32[]{:S(2)}) collective-permute-start(f32[1,4,96,512]{3,2,1,0:T(8,128)S(1)} %collective-permute-done.10), channel_id=1, source_target_pairs={{4,0},{8,4},{12,8},{16,12},{20,16},{24,20},{28,24},{32,28},{36,32}... | collective-permute-start | bytes 2359304 | tf_op jit(solution)/shard_map/ppermute | solution.py:26
  160.1 21.2 %copy-start.8 = (f32[1,4,96,512]{3,2,1,0:T(8,128)}, f32[1,4,96,512]{3,2,1,0:T(8,128)S(1)}, u32[]{:S(2)}) copy-start(f32[1,4,96,512]{3,2,1,0:T(8,128)S(1)} %collective-permute-done.4) | copy-start | bytes 2359300
  160.1 18.7 %collective-permute-start.5 = (f32[1,4,96,512]{3,2,1,0:T(8,128)S(1)}, f32[1,4,96,512]{3,2,1,0:T(8,128)S(1)}, u32[]{:S(2)}, u32[]{:S(2)}) collective-permute-start(f32[1,4,96,512]{3,2,1,0:T(8,128)S(1)} %collective-permute-done.4), channel_id=1, source_target_pairs={{0,4},{4,8},{8,12},{12,16},{16,20},{20,24},{24,28},{28,32},{32,36}... | collective-permute-start | bytes 2359304 | tf_op jit(solution)/shard_map/ppermute | solution.py:24
  162.9 18.4 %collective-permute-start.12 = (f32[1,4,96,512]{3,2,1,0:T(8,128)S(1)}, f32[1,4,96,512]{3,2,1,0:T(8,128)}, u32[]{:S(2)}, u32[]{:S(2)}) collective-permute-start(f32[1,4,96,512]{3,2,1,0:T(8,128)S(1)} %collective-permute-done.11), channel_id=1, source_target_pairs={{4,0},{8,4},{12,8},{16,12},{20,16},{24,20},{28,24},{32,28},{36,32}... | collective-permute-start | bytes 2359304 | tf_op jit(solution)/shard_map/ppermute | solution.py:26
  178.8 10.1 %copy-start.9 = (f32[1,4,96,512]{3,2,1,0:T(8,128)}, f32[1,4,96,512]{3,2,1,0:T(8,128)S(1)}, u32[]{:S(2)}) copy-start(f32[1,4,96,512]{3,2,1,0:T(8,128)S(1)} %collective-permute-done.5) | copy-start | bytes 2359300
  178.8 17.9 %collective-permute-start.6 = (f32[1,4,96,512]{3,2,1,0:T(8,128)S(1)}, f32[1,4,96,512]{3,2,1,0:T(8,128)}, u32[]{:S(2)}, u32[]{:S(2)}) collective-permute-start(f32[1,4,96,512]{3,2,1,0:T(8,128)S(1)} %collective-permute-done.5), channel_id=1, source_target_pairs={{0,4},{4,8},{8,12},{12,16},{16,20},{20,24},{24,28},{28,32},{32,36}... | collective-permute-start | bytes 2359304 | tf_op jit(solution)/shard_map/ppermute | solution.py:24
  181.3 17.9 %collective-permute-start.13 = (f32[1,4,96,512]{3,2,1,0:T(8,128)}, f32[1,4,96,512]{3,2,1,0:T(8,128)}, u32[]{:S(2)}, u32[]{:S(2)}) collective-permute-start(f32[1,4,96,512]{3,2,1,0:T(8,128)} %collective-permute-done.12), channel_id=1, source_target_pairs={{4,0},{8,4},{12,8},{16,12},{20,16},{24,20},{28,24},{32,28},{36,32}... | collective-permute-start | bytes 2359304 | tf_op jit(solution)/shard_map/ppermute | solution.py:26
  196.7 17.2 %collective-permute-start.7 = (f32[1,4,96,512]{3,2,1,0:T(8,128)}, f32[1,4,96,512]{3,2,1,0:T(8,128)}, u32[]{:S(2)}, u32[]{:S(2)}) collective-permute-start(f32[1,4,96,512]{3,2,1,0:T(8,128)} %collective-permute-done.6), channel_id=1, source_target_pairs={{0,4},{4,8},{8,12},{12,16},{16,20},{20,24},{24,28},{28,32},{32,36}... | collective-permute-start | bytes 2359304 | tf_op jit(solution)/shard_map/ppermute | solution.py:24
  198.6 32.6 %copy-start.3 = (f32[1,4,96,512]{3,2,1,0:T(8,128)S(1)}, f32[1,4,96,512]{3,2,1,0:T(8,128)}, u32[]{:S(2)}) copy-start(f32[1,4,96,512]{3,2,1,0:T(8,128)} %copy-done.2) | copy-start | bytes 2359300
  198.6 33.6 %copy-start.5 = (f32[1,4,96,512]{3,2,1,0:T(8,128)S(1)}, f32[1,4,96,512]{3,2,1,0:T(8,128)}, u32[]{:S(2)}) copy-start(f32[1,4,96,512]{3,2,1,0:T(8,128)} %copy-done.4) | copy-start | bytes 2359300
  198.6 34.6 %copy-start.7 = (f32[1,4,96,512]{3,2,1,0:T(8,128)S(1)}, f32[1,4,96,512]{3,2,1,0:T(8,128)}, u32[]{:S(2)}) copy-start(f32[1,4,96,512]{3,2,1,0:T(8,128)} %copy-done.6) | copy-start | bytes 2359300
  199.2 39.0 %collective-permute-start.14 = (f32[1,4,96,512]{3,2,1,0:T(8,128)}, f32[1,4,96,512]{3,2,1,0:T(8,128)S(1)}, u32[]{:S(2)}, u32[]{:S(2)}) collective-permute-start(f32[1,4,96,512]{3,2,1,0:T(8,128)} %collective-permute-done.13), channel_id=1, source_target_pairs={{4,0},{8,4},{12,8},{16,12},{20,16},{24,20},{28,24},{32,28},{36,32}... | collective-permute-start | bytes 2359304 | tf_op jit(solution)/shard_map/ppermute | solution.py:26
  249.6 403.7 %copy-start.1 = (f32[144,1536]{1,0:T(8,128)S(1)}, f32[144,1536]{1,0:T(8,128)}, u32[]{:S(2)}) copy-start(f32[144,1536]{1,0:T(8,128)} %param.5) | copy-start | bytes 2654212
  (2 other events, 1.8 us)
Sparse Core Ops, SparseCore 0:
  269.1 381.2 all-reduce.2
